TPU v7x, 32 devices: a whole 2x2x4 slice. The times are simulated.
32 devices in a mesh: dp: 8 (over z, y), mp: 4 (over x, core).
Axes of the slice: x: 2, y: 2, z: 4, core: 2. Of those that a mesh axis runs over, the one named last changes fastest.
Arguments:
- inputs: float32 [7168, 2304], P(('dp', 'mp')), may hold values from -16 to 16
- out_grad: float32 [7168, 2304], P(('dp', 'mp')), may hold values from -6 to 6
- segment_ids: int32 [8, 896], P('dp'), may hold values from 0 to 13, never falling along the last dimension, each value on 1 to 448 neighbouring positions
- pad_mask: int32 [8, 896], P('dp'), may hold values 0 or 1
- bit_sel: int32 [3], replicated, may hold values from 0 to 2
- w_qo: float32 [2, 2304, 2048], P(None, 'dp', 'mp'), may hold values from -1 to 1
- w_kv: float32 [2, 2304, 1024], P(None, 'dp', 'mp'), may hold values from -1 to 1
- w_mlp: float32 [3, 2304, 9216], P(None, 'dp', 'mp'), may hold values from -1 to 1
- norm_gains: float32 [9216], P(('dp', 'mp')), may hold values from -0.32 to 0.32
- m_qo: float32 [2, 2304, 2048], P(None, 'dp', 'mp'), may hold values from -0.3125 to 0.3125
- m_kv: float32 [2, 2304, 1024], P(None, 'dp', 'mp'), may hold values from -0.3125 to 0.3125
- m_mlp: float32 [3, 2304, 9216], P(None, 'dp', 'mp'), may hold values from -0.3125 to 0.3125
- m_gains: float32 [9216], P(('dp', 'mp')), may hold values from -0.3125 to 0.3125
- v_qo: float32 [2, 2304, 2048], P(None, 'dp', 'mp'), may hold values from 0.0066 to 0.105
- v_kv: float32 [2, 2304, 1024], P(None, 'dp', 'mp'), may hold values from 0.0066 to 0.105
- v_mlp: float32 [3, 2304, 9216], P(None, 'dp', 'mp'), may hold values from 0.0066 to 0.105
- v_gains: float32 [9216], P(('dp', 'mp')), may hold values from 0.0066 to 0.105
Outputs:
- outputs: float32 [7168, 2304], P(('dp', 'mp'))
- grad_in: float32 [7168, 2304], P(('dp', 'mp'))
- grad_norm: float32 [1], replicated
- new_w_qo: float32 [2, 2304, 2048], P(None, 'dp', 'mp')
- new_w_kv: float32 [2, 2304, 1024], P(None, 'dp', 'mp')
- new_w_mlp: float32 [3, 2304, 9216], P(None, 'dp', 'mp')
- new_gains: float32 [9216], P(('dp', 'mp'))
- new_m_qo: float32 [2, 2304, 2048], P(None, 'dp', 'mp')
- new_m_kv: float32 [2, 2304, 1024], P(None, 'dp', 'mp')
- new_m_mlp: float32 [3, 2304, 9216], P(None, 'dp', 'mp')
- new_m_gains: float32 [9216], P(('dp', 'mp'))
- new_v_qo: float32 [2, 2304, 2048], P(None, 'dp', 'mp')
- new_v_kv: float32 [2, 2304, 1024], P(None, 'dp', 'mp')
- new_v_mlp: float32 [3, 2304, 9216], P(None, 'dp', 'mp')
- new_v_gains: float32 [9216], P(('dp', 'mp'))
Inputs may be any that keep to these rules, and one draw needn't show every extreme that they name: `segment_ids`: ids never fall along a sequence; a document holds 1 to 448 slots, one exactly that many in each sequence.
All inputs are finite; a program needn't handle non-finite values. No bound on the sum of `pad_mask` on one device may be relied on, other than what follows from the above.
Results may differ from a plain program's by a relative error of at most 0.02.
Values may be sent and summed in bfloat16 or wider, within the bound.
A program may use at most 320 MiB of HBM per device.

v0:
```python
import math
import jax
import jax.numpy as jnp
from jax import lax
from jax.sharding import PartitionSpec as P

D = 2304
HEAD_WIDTH = 256
FF = 9216
NORMS = 4
QW = 2048
PARAMS = 77865984
EPSILON = 1e-06
SOFT_CAP = 50.0
ROPE_BASE = 10000.0
MASKED_SCORE = -1e30
FIRST_DECAY = 0.9
SECOND_DECAY = 0.95
LEARN_RATE = 0.04
WEIGHT_DECAY = 0.1
ADAM_EPSILON = 1e-08
CLIP_SCALE = 0.5


def quantize(master, fan_list, selector):
    shifts = jnp.where(selector == 0, 0, jnp.where(selector == 1, 4, 6)).astype(jnp.int32)
    spacing = jnp.left_shift(jnp.int32(1), shifts)
    step_sizes = jnp.array(
        [1.0 / (32.0 * math.sqrt(fan_in)) for fan_in in fan_list], jnp.float32
    ).reshape(-1, 1, 1)
    codes = jnp.clip(jnp.floor(master / step_sizes + 0.5), -128.0, 127.0).astype(jnp.int32)
    sliced = jnp.floor_divide(codes + spacing // 2, spacing)
    sliced = jnp.clip(sliced, -(128 // spacing), 128 // spacing - 1)
    return ((sliced * spacing).astype(jnp.float32) * step_sizes).astype(jnp.bfloat16)


def rms_norm(values, norm_gain):
    return (
        values
        * lax.rsqrt(jnp.mean(values * values, axis=-1, keepdims=True) + EPSILON)
        * (1.0 + norm_gain)
    )


def doc_positions(segments):
    slot_index = jnp.arange(segments.shape[0], dtype=jnp.int32)
    previous = jnp.concatenate([segments[:1] - 1, segments[:-1]])
    starts = segments != previous
    doc_begin = lax.cummax(jnp.where(starts, slot_index, 0), axis=0)
    return slot_index - doc_begin


def allowed_pairs(segments, padding):
    slot_index = jnp.arange(segments.shape[0], dtype=jnp.int32)
    same_doc = segments[:, None] == segments[None, :]
    causal = slot_index[None, :] <= slot_index[:, None]
    live_key = (padding[None, :] == 1) | (slot_index[None, :] == slot_index[:, None])
    return same_doc & causal & live_key


def apply_rotation(values, token_positions):
    half_dim = HEAD_WIDTH // 2
    frequency = ROPE_BASE ** (-jnp.arange(half_dim, dtype=jnp.float32) * 2.0 / HEAD_WIDTH)
    angles = token_positions.astype(jnp.float32)[:, None] * frequency[None, :]
    angles = jnp.concatenate([angles, angles], -1)
    cosine = jnp.cos(angles)[:, None, :]
    sine = jnp.sin(angles)[:, None, :]
    first_half = values[..., :half_dim]
    second = values[..., half_dim:]
    turned = jnp.concatenate([-second, first_half], -1)
    return values * cosine + turned * sine


def contract_rows(left, right):
    return lax.dot_general(
        left, right, (((0,), (0,)), ((), ())), preferred_element_type=jnp.float32
    )


def contract_cols(left, right):
    return lax.dot_general(
        left, right, (((1,), (1,)), ((), ())), preferred_element_type=jnp.float32
    )


def adam_update(master, first_moment, second_moment, gradient, factor):
    clipped = gradient * factor
    new_first = FIRST_DECAY * first_moment + (1.0 - FIRST_DECAY) * clipped
    new_second = SECOND_DECAY * second_moment + (1.0 - SECOND_DECAY) * clipped * clipped
    new_master = master - LEARN_RATE * (
        new_first / (jnp.sqrt(new_second) + ADAM_EPSILON) + WEIGHT_DECAY * master
    )
    return (new_master, new_first, new_second)


def local(
    inputs,
    out_grad,
    segment_ids,
    pad_mask,
    bit_sel,
    w_qo,
    w_kv,
    w_mlp,
    norm_gains,
    m_qo,
    m_kv,
    m_mlp,
    m_gains,
    v_qo,
    v_kv,
    v_mlp,
    v_gains,
):
    row_count = inputs.shape[0]
    seq_len = segment_ids.shape[1]
    low_qo = quantize(w_qo, (D, QW), bit_sel[0])
    low_kv = quantize(w_kv, (D, D), bit_sel[1])
    low_mlp = quantize(w_mlp, (D, D, FF), bit_sel[2])
    full_qo, full_kv, full_mlp = (
        lax.all_gather(low_qo, "dp", axis=1, tiled=True),
        lax.all_gather(low_kv, "dp", axis=1, tiled=True),
        lax.all_gather(low_mlp, "dp", axis=1, tiled=True),
    )
    gain_rows = lax.all_gather(norm_gains, ("dp", "mp"), axis=0, tiled=True).reshape(NORMS, D)
    segments = segment_ids[0]
    padding = pad_mask[0]
    token_positions = doc_positions(segments)
    allowed = allowed_pairs(segments, padding)
    local_heads = full_qo.shape[2] // HEAD_WIDTH
    kv_heads = full_kv.shape[2] // HEAD_WIDTH
    group_size = local_heads // kv_heads
    scale = HEAD_WIDTH ** (-0.5)
    normalized_rows = rms_norm(inputs, gain_rows[0]).astype(jnp.bfloat16)
    seq_normed = lax.all_gather(normalized_rows, "mp", axis=0, tiled=True)
    query_linear = jnp.dot(seq_normed, full_qo[0], preferred_element_type=jnp.float32)
    key_linear = jnp.dot(seq_normed, full_kv[0], preferred_element_type=jnp.float32)
    value_lin = jnp.dot(seq_normed, full_kv[1], preferred_element_type=jnp.float32)

    def rope_query(values):
        turned = apply_rotation(values.reshape(seq_len, local_heads, HEAD_WIDTH), token_positions)
        return turned.reshape(seq_len, kv_heads, group_size, HEAD_WIDTH)

    def rope_key(values):
        return apply_rotation(values.reshape(seq_len, kv_heads, HEAD_WIDTH), token_positions)

    query_bf = rope_query(query_linear).astype(jnp.bfloat16)
    key_bf = rope_key(key_linear).astype(jnp.bfloat16)
    value_bf = value_lin.astype(jnp.bfloat16).reshape(seq_len, kv_heads, HEAD_WIDTH)

    def masked_scores():
        raw_scores = (
            jnp.einsum("qkgd,pkd->kgqp", query_bf, key_bf, preferred_element_type=jnp.float32)
            * scale
        )
        capped = jnp.where(
            allowed[None, None], SOFT_CAP * jnp.tanh(raw_scores / SOFT_CAP), MASKED_SCORE
        )
        return (raw_scores, capped)

    raw_scores, capped = masked_scores()
    row_top = jnp.max(capped, axis=-1, keepdims=True)
    log_total = row_top + jnp.log(jnp.sum(jnp.exp(capped - row_top), axis=-1, keepdims=True))
    probs_bf = jnp.exp(capped - log_total).astype(jnp.bfloat16)
    mixed_bf = (
        jnp.einsum("kgqp,pkd->qkgd", probs_bf, value_bf, preferred_element_type=jnp.float32)
        .reshape(seq_len, -1)
        .astype(jnp.bfloat16)
    )
    row_block = mixed_bf
    attended = lax.psum_scatter(
        contract_cols(row_block, full_qo[1]), "mp", scatter_dimension=0, tiled=True
    )
    hidden_in = inputs + rms_norm(attended, gain_rows[1])
    ffn_normed = rms_norm(hidden_in, gain_rows[2]).astype(jnp.bfloat16)
    seq_ffn = lax.all_gather(ffn_normed, "mp", axis=0, tiled=True)
    gate_up = jnp.einsum("td,kdf->ktf", seq_ffn, full_mlp[:2], preferred_element_type=jnp.float32)
    activated_bf = (jax.nn.gelu(gate_up[0], approximate=True) * gate_up[1]).astype(jnp.bfloat16)
    row_block = activated_bf
    branch = lax.psum_scatter(
        contract_cols(row_block, full_mlp[2]), "mp", scatter_dimension=0, tiled=True
    )
    outputs = hidden_in + rms_norm(branch, gain_rows[3])
    row_live = lax.dynamic_slice_in_dim(
        padding, lax.axis_index("mp") * row_count, row_count
    ).astype(jnp.float32)
    cotangent = out_grad * row_live[:, None]
    _, branch_pull = jax.vjp(rms_norm, branch, gain_rows[3])
    grad_branch, grad_gain_three = branch_pull(cotangent)
    seq_grad_branch = lax.all_gather(grad_branch.astype(jnp.bfloat16), "mp", axis=0, tiled=True)
    back_qo, back_kv, back_mlp = (
        lax.all_gather(low_qo, "dp", axis=1, tiled=True),
        lax.all_gather(low_kv, "dp", axis=1, tiled=True),
        lax.all_gather(low_mlp, "dp", axis=1, tiled=True),
    )
    grad_act = jnp.dot(seq_grad_branch, back_mlp[2], preferred_element_type=jnp.float32)
    grad_down = contract_rows(seq_grad_branch, activated_bf)
    _, act_pull = jax.vjp(
        lambda gate_in, up_in: jax.nn.gelu(gate_in, approximate=True) * up_in,
        gate_up[0],
        gate_up[1],
    )
    grad_gate, grad_up = act_pull(grad_act)
    grad_gate_up = jnp.stack([grad_gate, grad_up]).astype(jnp.bfloat16)
    grad_gate_up_w = jnp.einsum(
        "ktf,td->kdf", grad_gate_up, seq_ffn, preferred_element_type=jnp.float32
    )
    row_block = grad_gate_up
    grad_ffn_normed = lax.psum_scatter(
        jnp.einsum("ktf,kdf->td", row_block, back_mlp[:2], preferred_element_type=jnp.float32),
        "mp",
        scatter_dimension=0,
        tiled=True,
    )
    _, ffn_pull = jax.vjp(rms_norm, hidden_in, gain_rows[2])
    grad_hidden_part, grad_gain_two = ffn_pull(grad_ffn_normed)
    grad_hidden = cotangent + grad_hidden_part
    _, attn_pull = jax.vjp(rms_norm, attended, gain_rows[1])
    grad_attended, grad_gain_one = attn_pull(grad_hidden)
    seq_grad_attended = lax.all_gather(grad_attended.astype(jnp.bfloat16), "mp", axis=0, tiled=True)
    grad_mixed = jnp.dot(seq_grad_attended, back_qo[1], preferred_element_type=jnp.float32)
    grad_mixed = grad_mixed.astype(jnp.bfloat16).reshape(seq_len, kv_heads, group_size, HEAD_WIDTH)
    grad_out_w = contract_rows(seq_grad_attended, mixed_bf)
    raw_scores, capped = masked_scores()
    probs = jnp.exp(capped - log_total)
    probs_bf = probs.astype(jnp.bfloat16)
    grad_value = jnp.einsum(
        "kgqp,qkgd->pkd", probs_bf, grad_mixed, preferred_element_type=jnp.float32
    )
    grad_probs = jnp.einsum(
        "qkgd,pkd->kgqp", grad_mixed, value_bf, preferred_element_type=jnp.float32
    )
    inner_sum = jnp.sum(probs * grad_probs, axis=-1, keepdims=True)
    grad_capped = probs * (grad_probs - inner_sum)
    grad_raw = (grad_capped * (1.0 - jnp.square(jnp.tanh(raw_scores / SOFT_CAP)))).astype(
        jnp.bfloat16
    )
    grad_query = (
        jnp.einsum("kgqp,pkd->qkgd", grad_raw, key_bf, preferred_element_type=jnp.float32) * scale
    )
    grad_key = (
        jnp.einsum("kgqp,qkgd->pkd", grad_raw, query_bf, preferred_element_type=jnp.float32) * scale
    )
    _, query_pull = jax.vjp(rope_query, query_linear)
    grad_query_lin = query_pull(grad_query)[0].astype(jnp.bfloat16)
    _, key_pull = jax.vjp(rope_key, key_linear)
    grad_key_lin = key_pull(grad_key)[0].astype(jnp.bfloat16)
    grad_value_lin = grad_value.reshape(seq_len, -1).astype(jnp.bfloat16)
    grad_query_w = contract_rows(seq_normed, grad_query_lin)
    grad_key_w = contract_rows(seq_normed, grad_key_lin)
    grad_value_w = contract_rows(seq_normed, grad_value_lin)
    grad_normed = lax.psum_scatter(
        contract_cols(grad_query_lin, back_qo[0])
        + contract_cols(grad_key_lin, back_kv[0])
        + contract_cols(grad_value_lin, back_kv[1]),
        "mp",
        scatter_dimension=0,
        tiled=True,
    )
    _, input_pull = jax.vjp(rms_norm, inputs, gain_rows[0])
    grad_input_part, grad_gain_zero = input_pull(grad_normed)
    grad_in = grad_hidden + grad_input_part
    sum_qo, sum_kv, sum_mlp = (
        lax.psum_scatter(
            jnp.stack([grad_query_w, grad_out_w]).astype(jnp.bfloat16),
            "dp",
            scatter_dimension=1,
            tiled=True,
        ).astype(jnp.float32),
        lax.psum_scatter(
            jnp.stack([grad_key_w, grad_value_w]).astype(jnp.bfloat16),
            "dp",
            scatter_dimension=1,
            tiled=True,
        ).astype(jnp.float32),
        lax.psum_scatter(
            jnp.concatenate([grad_gate_up_w, grad_down[None]], 0).astype(jnp.bfloat16),
            "dp",
            scatter_dimension=1,
            tiled=True,
        ).astype(jnp.float32),
    )
    gain_terms = jnp.stack([grad_gain_zero, grad_gain_one, grad_gain_two, grad_gain_three]).reshape(
        -1
    )
    sum_gains = lax.psum_scatter(gain_terms, ("dp", "mp"), scatter_dimension=0, tiled=True)
    local_squares = (
        jnp.sum(sum_qo * sum_qo)
        + jnp.sum(sum_kv * sum_kv)
        + jnp.sum(sum_mlp * sum_mlp)
        + jnp.sum(sum_gains * sum_gains)
    )
    grad_norm = jnp.sqrt(lax.psum(local_squares, ("dp", "mp")))
    factor = jnp.minimum(1.0, CLIP_SCALE * math.sqrt(PARAMS) / grad_norm)
    new_w_qo, new_m_qo, new_v_qo = adam_update(w_qo, m_qo, v_qo, sum_qo, factor)
    new_w_kv, new_m_kv, new_v_kv = adam_update(w_kv, m_kv, v_kv, sum_kv, factor)
    new_w_mlp, new_m_mlp, new_v_mlp = adam_update(w_mlp, m_mlp, v_mlp, sum_mlp, factor)
    new_gains, new_m_gains, new_v_gains = adam_update(
        norm_gains, m_gains, v_gains, sum_gains, factor
    )
    return (
        outputs,
        grad_in,
        grad_norm.reshape(1),
        new_w_qo,
        new_w_kv,
        new_w_mlp,
        new_gains,
        new_m_qo,
        new_m_kv,
        new_m_mlp,
        new_m_gains,
        new_v_qo,
        new_v_kv,
        new_v_mlp,
        new_v_gains,
    )


def solution(mesh):
    placed = (
        P(("dp", "mp"), None),
        P(("dp", "mp"), None),
        P("dp", None),
        P("dp", None),
        P(),
        P(None, "dp", "mp"),
        P(None, "dp", "mp"),
        P(None, "dp", "mp"),
        P(("dp", "mp")),
        P(None, "dp", "mp"),
        P(None, "dp", "mp"),
        P(None, "dp", "mp"),
        P(("dp", "mp")),
        P(None, "dp", "mp"),
        P(None, "dp", "mp"),
        P(None, "dp", "mp"),
        P(("dp", "mp")),
    )
    return jax.shard_map(
        local,
        mesh=mesh,
        in_specs=placed,
        out_specs=(
            P(("dp", "mp"), None),
            P(("dp", "mp"), None),
            P(),
            P(None, "dp", "mp"),
            P(None, "dp", "mp"),
            P(None, "dp", "mp"),
            P(("dp", "mp")),
            P(None, "dp", "mp"),
            P(None, "dp", "mp"),
            P(None, "dp", "mp"),
            P(("dp", "mp")),
            P(None, "dp", "mp"),
            P(None, "dp", "mp"),
            P(None, "dp", "mp"),
            P(("dp", "mp")),
        ),
        check_vma=False,
    )
```

profile of v0, /device:TPU:0, one launch (start us, length us, event | category | flops | bytes accessed | tf_op | source)
XLA Modules:
  0.0 2190.6 jit_solution(6801145849870063751)
XLA Ops:
  10.1 7.8 fusion.135
  18.9 43.8 %all-reduce.4 = f32[9216]{0:T(1024)S(1)} all-reduce(f32[9216]{0:T(1024)S(1)} %dynamic-update-slice), channel_id=1, replica_groups=mesh['dp'=8,'mp'=4] {'dp','mp'}, use_global_device_ids=true, to_apply=%add.4 | all-reduce | flops 9216 | bytes 73728
  62.7 1.8 multiply_reduce_fusion.11
  68.5 13.4 fusion.107
  84.8 2.2 fusion.70
  87.0 21.4 all-gather.8.cloned.1.call-done
  108.4 4.1 fusion.115
  112.6 4.6 fusion.117
  117.2 2.0 fusion.98
  119.3 71.8 %all-gather.12.cloned.1.call-done = bf16[2,2304,512]{2,1,0:T(8,128)(2,1)} async-done(((bf16[2,288,512]{2,1,0:T(8,128)(2,1)}), bf16[2,2304,512]{2,1,0:T(8,128)(2,1)}) %all-gather.12.cloned.1.call-update) | async-done | bytes 4718608 | tf_op jit(solution)/shard_map/all_gather | solution.py:121
  191.1 3.2 slice_bitcast_fusion.6
  194.3 4.3 copy.65
  198.6 5.5 fusion.52
  205.7 2.0 fusion.63
  207.7 2.0 exponential_reduce_fusion
  209.8 2.4 convolution_convert_fusion.6
  212.4 5.6 fusion.75
  218.1 69.1 %reduce-scatter.8.cloned.1.call-done = f32[224,2304]{1,0:T(8,128)} async-done(((f32[896,2304]{1,0:T(8,128)}), f32[224,2304]{1,0:T(8,128)}) %reduce-scatter.8.cloned.1.call-update) | async-done | bytes 2064400 | tf_op jit(solution)/shard_map/reduce_scatter | solution.py:171
  287.3 1.8 multiply_reduce_fusion.10
  289.1 2.1 multiply_reduce_fusion.9
  295.2 84.8 %fusion.33 = bf16[3,288,2304]{2,1,0:T(8,128)(2,1)} fusion(f32[3,288,2304]{2,1,0:T(8,128)} %param.27, f32[3]{0:T(128)S(1)} %copy-done.54, s32[]{:T(128)} %bitcast.23, s32[]{:T(128)S(6)} %sign.50, s32[]{:T(128)S(6)} %select_n.93, f32[3]{0:T(128)S(1)} %copy-done.55, s32[]{:T(128)S(6)} %neg.36, s32[]{:T(128)S(6)} %sub.130), kind=kLoop, calls=%fused_computation.52 | loop fusion | flops 39813120 | bytes 11943980 | tf_op jit(solution)/shard_map/convert_element_type | solution.py:34
  380.1 605.9 %all-gather.14.cloned.1.call-done = bf16[3,2304,2304]{2,1,0:T(8,128)(2,1)} async-done(((bf16[3,288,2304]{2,1,0:T(8,128)(2,1)}), bf16[3,2304,2304]{2,1,0:T(8,128)(2,1)}) %all-gather.14.cloned.1.call-update) | async-done | bytes 31850512 | tf_op jit(solution)/shard_map/all_gather | solution.py:123
  985.9 28.7 %convolution_bitcast_fusion = f32[2,896,2304]{1,2,0:T(8,128)} fusion(bf16[3,2304,2304]{2,1,0:T(8,128)(2,1)} %all-gather.14.cloned.1.call-done, bf16[896,2304]{1,0:T(8,128)(2,1)} %all-gather.16.cloned.1.call-done), kind=kOutput, calls=%fused_computation.18 | convolution fusion | flops 19025362944 | bytes 52494336 | tf_op jit(solution)/shard_map/td,kdf->ktf/dot_general | solution.py:177
  1014.7 22.6 %fusion.6 = f32[896,2304]{1,0:T(8,128)} fusion(bf16[3,2304,2304]{2,1,0:T(8,128)(2,1)} %all-gather.14.cloned.1.call-done, f32[2,896,2304]{1,2,0:T(8,128)} %convolution_bitcast_fusion), kind=kOutput, calls=%fused_computation.17 | convolution fusion | flops 9533325312 | bytes 35389440 | tf_op jit(solution)/shard_map/dot_general | solution.py:81
  1037.4 70.9 %reduce-scatter.10.cloned.1.call-done = f32[224,2304]{1,0:T(8,128)} async-done(((f32[896,2304]{1,0:T(8,128)}), f32[224,2304]{1,0:T(8,128)}) %reduce-scatter.10.cloned.1.call-update) | async-done | bytes 2064400 | tf_op jit(solution)/shard_map/reduce_scatter | solution.py:180
  1108.3 1.9 multiply_reduce_fusion.8
  1110.3 3.5 multiply_reduce_fusion
  1113.8 2.6 fusion.77
  1116.5 34.2 %all-gather.18.cloned.1.call-done = bf16[896,2304]{1,0:T(8,128)(2,1)} async-done(((bf16[224,2304]{1,0:T(8,128)(2,1)}), bf16[896,2304]{1,0:T(8,128)(2,1)}) %all-gather.18.cloned.1.call-update) | async-done | bytes 4128784 | tf_op jit(solution)/shard_map/all_gather | solution.py:190
  1150.7 26.8 %fusion.58 = (bf16[1,896,2304]{1,2,0:T(8,128)(2,1)}, bf16[1,896,2304]{1,2,0:T(8,128)(2,1)}) fusion(f32[2,896,2304]{1,2,0:T(8,128)} %convolution_bitcast_fusion, bf16[896,2304]{1,0:T(8,128)(2,1)} %all-gather.18.cloned.1.call-done, bf16[3,2304,2304]{2,1,0:T(8,128)(2,1)} %all-gather.14.cloned.1.call-done), kind=kOutput, calls=%fused_computation.87 | convolution fusion | flops 9562226688 | bytes 39518208 | tf_op jit(solution)/shard_map/dot_general | solution.py:196
  1177.5 27.1 %fusion.43 = f32[896,2304]{1,0:T(8,128)} fusion(bf16[3,2304,2304]{2,1,0:T(8,128)(2,1)} %all-gather.14.cloned.1.call-done, bf16[1,896,2304]{1,2,0:T(8,128)(2,1)} %get-tuple-element.39, bf16[1,896,2304]{1,2,0:T(8,128)(2,1)} %get-tuple-element.38), kind=kOutput, calls=%fused_computation.73 | convolution fusion | flops 19029491712 | bytes 37748736 | tf_op jit(solution)/shard_map/ktf,kdf->td/dot_general | solution.py:210
  1204.7 71.0 %reduce-scatter.12.cloned.1.call-done = f32[224,2304]{1,0:T(8,128)} async-done(((f32[896,2304]{1,0:T(8,128)}), f32[224,2304]{1,0:T(8,128)}) %reduce-scatter.12.cloned.1.call-update) | async-done | bytes 2064400 | tf_op jit(solution)/shard_map/reduce_scatter | solution.py:209
  1275.7 2.2 multiply_reduce_fusion.1
  1278.5 2.9 multiply_reduce_fusion.2
  1284.2 34.2 %all-gather.20.cloned.1.call-done = bf16[896,2304]{1,0:T(8,128)(2,1)} async-done(((bf16[224,2304]{1,0:T(8,128)(2,1)}), bf16[896,2304]{1,0:T(8,128)(2,1)}) %all-gather.20.cloned.1.call-update) | async-done | bytes 4128784 | tf_op jit(solution)/shard_map/all_gather | solution.py:220
  1318.4 5.6 fusion.86
  1324.0 5.5 fusion.41
  1329.6 5.5 fusion.99
  1335.1 2.9 fusion.40
  1338.0 3.8 fusion.126
  1341.9 3.6 fusion.125
  1348.5 1.6 pad_maximum_fusion.5
  1350.1 2.5 bitcast_multiply_fusion.7
  1355.3 2.9 fusion.60
  1358.2 2.9 fusion.59
  1361.2 2.6 pad_maximum_fusion.4
  1366.9 4.1 fusion.72
  1371.0 4.5 add_add_fusion
  1375.6 20.8 fusion.3
  1396.3 29.3 %fusion.2 = bf16[2,2304,2304]{2,1,0:T(8,128)(2,1)} fusion(bf16[1,896,2304]{1,2,0:T(8,128)(2,1)} %get-tuple-element.39, bf16[1,896,2304]{1,2,0:T(8,128)(2,1)} %get-tuple-element.38, bf16[896,2304]{1,0:T(8,128)(2,1)S(1)} %copy-done.61), kind=kOutput, calls=%fused_computation.4 | convolution fusion | flops 19052494848 | bytes 33619968 | tf_op jit(solution)/shard_map/ktf,td->kdf/dot_general | solution.py:205
  1425.6 22.0 %pad_maximum_fusion = bf16[3,2304,2304]{2,1,0:T(8,128)(2,1)} fusion(bf16[1,2304,2304]{2,1,0:T(8,128)(2,1)} %fusion.3, bf16[2,2304,2304]{2,1,0:T(8,128)(2,1)} %fusion.2), kind=kLoop, calls=%fused_computation | loop fusion | flops 15925248 | bytes 63700992 | tf_op jit(solution)/shard_map/concatenate | solution.py:277
  1448.5 1.7 fusion.129
  1450.2 67.4 %reduce-scatter.16.cloned.1.call-done = bf16[2,288,512]{2,1,0:T(8,128)(2,1)} async-done(((bf16[2,2304,512]{2,1,0:T(8,128)(2,1)}), bf16[2,288,512]{2,1,0:T(8,128)(2,1)}) %reduce-scatter.16.cloned.1.call-update) | async-done | bytes 589840 | tf_op jit(solution)/shard_map/reduce_scatter | solution.py:264
  1517.6 2.0 fusion.101
  1520.9 70.1 %reduce-scatter.14.cloned.1.call-done = f32[224,2304]{1,0:T(8,128)} async-done(((f32[896,2304]{1,0:T(8,128)}), f32[224,2304]{1,0:T(8,128)}) %reduce-scatter.14.cloned.1.call-update) | async-done | bytes 2064400 | tf_op jit(solution)/shard_map/reduce_scatter | solution.py:252
  1591.0 2.1 multiply_reduce_fusion.3
  1593.1 44.4 %all-reduce.5 = f32[9216]{0:T(1024)S(1)} all-reduce(f32[9216]{0:T(1024)S(1)} %reshape.540), channel_id=9, replica_groups=mesh['dp'=8,'mp'=4] {'dp','mp'}, use_global_device_ids=true, to_apply=%region_27.28.clone | all-reduce | flops 9216 | bytes 73728
  1638.3 470.0 %reduce-scatter.20.cloned.1.call-done = bf16[3,288,2304]{2,1,0:T(8,128)(2,1)} async-done(((bf16[3,2304,2304]{2,1,0:T(8,128)(2,1)}), bf16[3,288,2304]{2,1,0:T(8,128)(2,1)}) %reduce-scatter.20.cloned.1.call-update) | async-done | bytes 3981328 | tf_op jit(solution)/shard_map/reduce_scatter | solution.py:276
  2108.3 4.8 fusion.27
  2114.4 4.0 fusion.80
  2118.4 39.6 %psum.7 = f32[]{:T(128)} all-reduce(f32[]{:T(128)S(6)} %add.301), channel_id=1, replica_groups=mesh['dp'=8,'mp'=4] {'dp','mp'}, use_global_device_ids=true, to_apply=%region_29.30 | all-reduce | flops 1 | bytes 8 | tf_op jit(solution)/shard_map/psum | solution.py:293
  2159.5 4.6 multiply_subtract_fusion.1
  2164.1 2.7 multiply_subtract_fusion.2
  2166.8 15.6 multiply_subtract_fusion
  (221 shorter events, 26.5 us)
Async XLA Ops:
  7.2 61.3 %copy-start.56 = (f32[2]{0:T(128)S(1)}, f32[2]{0:T(128)}, u32[]{:S(2)}) copy-start(f32[2]{0:T(128)} %constant.220) | copy-start | bytes 28
  7.2 61.3 %copy-start.57 = (f32[2]{0:T(128)S(1)}, f32[2]{0:T(128)}, u32[]{:S(2)}) copy-start(f32[2]{0:T(128)} %constant.206.clone) | copy-start | bytes 28
  7.2 58.4 %copy-start = (f32[224,2304]{1,0:T(8,128)S(1)}, f32[224,2304]{1,0:T(8,128)}, u32[]{:S(2)}) copy-start(f32[224,2304]{1,0:T(8,128)} %param.20) | copy-start | bytes 6193156
  7.2 61.2 %copy-start.17 = (f32[2,288,512]{2,1,0:T(8,128)S(1)}, f32[2,288,512]{2,1,0:T(8,128)}, u32[]{:S(2)}) copy-start(f32[2,288,512]{2,1,0:T(8,128)} %param.25) | copy-start | bytes 3538948
  7.2 79.7 %all-gather.10.cloned.1.call-start = ((), (), s32[]{:S(2)}) async-start(), calls=%async_computation.8 | async-start | bytes 2654208 | tf_op jit(solution)/shard_map/all_gather | solution.py:122
  17.9 90.5 %all-gather.8.cloned.1.call-start = ((), (), s32[]{:S(2)}) async-start(), calls=%async_computation.7 | async-start | bytes 5160960 | tf_op jit(solution)/shard_map/all_gather | solution.py:135
  62.6 19.3 copy-start.43
  62.6 21.1 copy-start.51
  64.5 19.3 copy-start.39
  65.0 224.0 %copy-start.34 = (f32[2304]{0:T(1024)}, f32[2304]{0:T(1024)S(1)}, u32[]{:S(2)}) copy-start(f32[2304]{0:T(1024)S(1)} %get-tuple-element.55) | copy-start | bytes 27652
  66.9 124.2 %all-gather.12.cloned.1.call-start = ((), (), s32[]{:S(2)}) async-start(), calls=%async_computation.9 | async-start | bytes 5308416 | tf_op jit(solution)/shard_map/all_gather | solution.py:121
  81.9 205.4 %reduce-scatter.8.cloned.1.call-start = ((), (), s32[]{:S(2)}) async-start(), calls=%async_computation.10 | async-start | bytes 10321920 | tf_op jit(solution)/shard_map/reduce_scatter | solution.py:171
  108.4 8.8 copy-start.58
  112.5 4.7 copy-start.21
  117.2 87.1 %copy-start.11 = (f32[896,256]{0,1:T(8,128)}, f32[896,256]{0,1:T(8,128)S(1)}, u32[]{:S(2)}) copy-start(f32[896,256]{0,1:T(8,128)S(1)} %get-tuple-element.52) | copy-start | bytes 2752516
  207.7 4.5 copy-start.5
  207.7 4.6 slice-start.2
  212.2 5.9 copy-start.63
  218.1 162.0 %all-gather.16.cloned.1.call-start = ((), (), s32[]{:S(2)}) async-start(), calls=%async_computation.12 | async-start | bytes 5160960 | tf_op jit(solution)/shard_map/all_gather | solution.py:176
  289.1 4.7 copy-start.46
  289.1 4.7 copy-start.41
  289.1 6.1 copy-start.54
  289.1 6.1 copy-start.55
  291.2 88.7 %copy-start.48 = (f32[224]{0:T(256)}, f32[224]{0:T(256)S(1)}, u32[]{:S(2)}) copy-start(f32[224]{0:T(256)S(1)} %get-tuple-element.36) | copy-start | bytes 2692
  293.8 692.2 %all-gather.14.cloned.1.call-start = ((), (), s32[]{:S(2)}) async-start(), calls=%async_computation.11 | async-start | bytes 35831808 | tf_op jit(solution)/shard_map/all_gather | solution.py:123
  380.0 728.4 %reduce-scatter.10.cloned.1.call-start = ((), (), s32[]{:S(2)}) async-start(), calls=%async_computation.13 | async-start | bytes 10321920 | tf_op jit(solution)/shard_map/reduce_scatter | solution.py:180
  1037.3 76.5 %copy-start.3 = (f32[224,2304]{1,0:T(8,128)S(1)}, f32[224,2304]{1,0:T(8,128)}, u32[]{:S(2)}) copy-start(f32[224,2304]{1,0:T(8,128)} %copy-done.2) | copy-start | bytes 6193156
  1037.3 113.4 %all-gather.18.cloned.1.call-start = ((), (), s32[]{:S(2)}) async-start(), calls=%async_computation.14 | async-start | bytes 5160960 | tf_op jit(solution)/shard_map/all_gather | solution.py:190
  1108.3 5.5 copy-start.7
  1108.3 5.5 copy-start.8
  1116.4 159.2 %reduce-scatter.12.cloned.1.call-start = ((), (), s32[]{:S(2)}) async-start(), calls=%async_computation.15 | async-start | bytes 10321920 | tf_op jit(solution)/shard_map/reduce_scatter | solution.py:209
  1204.6 73.3 %copy-start.49 = (f32[224]{0:T(256)S(1)}, f32[224]{0:T(256)}, u32[]{:S(2)}) copy-start(f32[224]{0:T(256)} %copy-done.48) | copy-start | bytes 2692
  1204.6 73.3 %copy-start.35 = (f32[2304]{0:T(1024)S(1)}, f32[2304]{0:T(1024)}, u32[]{:S(2)}) copy-start(f32[2304]{0:T(1024)} %copy-done.34) | copy-start | bytes 27652
  1204.6 73.3 %copy-start.42 = (f32[224]{0:T(256)S(1)}, f32[224]{0:T(256)}, u32[]{:S(2)}) copy-start(f32[224]{0:T(256)} %copy-done.41) | copy-start | bytes 2692
  1204.7 113.8 %all-gather.20.cloned.1.call-start = ((), (), s32[]{:S(2)}) async-start(), calls=%async_computation.16 | async-start | bytes 5160960 | tf_op jit(solution)/shard_map/all_gather | solution.py:220
  1284.1 39.9 %copy-start.15 = (pred[896,896]{0,1:T(8,128)(4,1)S(1)}, pred[896,896]{0,1:T(8,128)(4,1)}, u32[]{:S(2)}) copy-start(pred[896,896]{0,1:T(8,128)(4,1)} %fusion.70) | copy-start | bytes 2408452
  1284.2 39.9 %copy-start.38 = (f32[2,896]{1,0:T(2,128)S(1)}, f32[2,896]{1,0:T(2,128)}, u32[]{:S(2)}) copy-start(f32[2,896]{1,0:T(2,128)} %copy-done.37) | copy-start | bytes 21508
  1284.2 39.8 %copy-start.66 = (bf16[896,256,1]{1,0,2:T(8,128)(2,1)S(1)}, bf16[896,256,1]{1,0,2:T(8,128)(2,1)}, u32[]{:S(2)}) copy-start(bf16[896,256,1]{1,0,2:T(8,128)(2,1)} %fusion.98) | copy-start | bytes 1376260
  1284.2 164.3 %reduce-scatter.18.cloned.1.call-start = ((), (), s32[]{:S(2)}) async-start(), calls=%async_computation.19 | async-start | bytes 2654208 | tf_op jit(solution)/shard_map/reduce_scatter | solution.py:270
  1324.0 11.1 slice-start
  1324.0 11.0 slice-start.1
  1329.6 5.5 copy-start.16
  1335.0 10.5 copy-start.30
  1335.1 2.9 copy-start.18
  1335.1 2.9 copy-start.20
  1338.0 7.5 copy-start.59
  1345.5 2.9 copy-start.24
  1350.1 167.5 %reduce-scatter.16.cloned.1.call-start = ((), (), s32[]{:S(2)}) async-start(), calls=%async_computation.18 | async-start | bytes 5308416 | tf_op jit(solution)/shard_map/reduce_scatter | solution.py:264
  1355.3 2.9 copy-start.28
  1355.3 2.9 copy-start.60
  1363.8 227.2 %reduce-scatter.14.cloned.1.call-start = ((), (), s32[]{:S(2)}) async-start(), calls=%async_computation.17 | async-start | bytes 10321920 | tf_op jit(solution)/shard_map/reduce_scatter | solution.py:252
  1366.8 4.1 copy-start.31
  1375.5 732.8 %reduce-scatter.20.cloned.1.call-start = ((), (), s32[]{:S(2)}) async-start(), calls=%async_computation.20 | async-start | bytes 35831808 | tf_op jit(solution)/shard_map/reduce_scatter | solution.py:276
  1375.6 20.8 copy-start.61
  1447.7 143.3 %copy-start.1 = (f32[224,2304]{1,0:T(8,128)S(1)}, f32[224,2304]{1,0:T(8,128)}, u32[]{:S(2)}) copy-start(f32[224,2304]{1,0:T(8,128)} %param.20) | copy-start | bytes 6193156
  1447.7 143.3 %copy-start.33 = (f32[2304]{0:T(1024)S(1)}, f32[2304]{0:T(1024)}, u32[]{:S(2)}) copy-start(f32[2304]{0:T(1024)} %copy-done.32) | copy-start | bytes 27652
  1447.7 143.3 %copy-start.40 = (f32[224]{0:T(256)S(1)}, f32[224]{0:T(256)}, u32[]{:S(2)}) copy-start(f32[224]{0:T(256)} %copy-done.39) | copy-start | bytes 2692
  1447.8 190.5 %copy-start.45 = (f32[224]{0:T(256)S(1)}, f32[224]{0:T(256)}, u32[]{:S(2)}) copy-start(f32[224]{0:T(256)} %copy-done.44) | copy-start | bytes 2692
  2114.3 44.4 %copy-start.50 = (f32[288]{0:T(512)S(1)}, f32[288]{0:T(512)}, u32[]{:S(2)}) copy-start(f32[288]{0:T(512)} %param.28) | copy-start | bytes 3460
  2114.4 44.4 %copy-start.52 = (f32[288]{0:T(512)S(1)}, f32[288]{0:T(512)}, u32[]{:S(2)}) copy-start(f32[288]{0:T(512)} %param.36) | copy-start | bytes 3460
  2114.4 44.4 %copy-start.53 = (f32[288]{0:T(512)S(1)}, f32[288]{0:T(512)}, u32[]{:S(2)}) copy-start(f32[288]{0:T(512)} %param.32) | copy-start | bytes 3460
  2118.4 45.7 %copy-start.23 = (f32[2,288,256]{2,1,0:T(8,128)S(1)}, f32[2,288,256]{2,1,0:T(8,128)}, u32[]{:S(2)}) copy-start(f32[2,288,256]{2,1,0:T(8,128)} %param.26) | copy-start | bytes 1769476
  2118.4 45.7 %copy-start.27 = (bf16[2,288,256]{2,1,0:T(8,128)(2,1)S(1)}, bf16[2,288,256]{2,1,0:T(8,128)(2,1)}, u32[]{:S(2)}) copy-start(bf16[2,288,256]{2,1,0:T(8,128)(2,1)} %reduce-scatter.18.cloned.1.call-done) | copy-start | bytes 884740
  2159.5 7.4 copy-start.10
  (21 other events, 36.7 us)
Sparse Core Ops, SparseCore 0:
  18.0 55.5 all-gather.9
  75.7 32.6 all-gather.7
  111.2 79.8 all-gather.11
  218.2 69.0 reduce-scatter.7
  293.9 34.1 all-gather.15
  380.1 605.7 all-gather.13
  1037.4 70.8 reduce-scatter.9
  1116.6 34.0 all-gather.17
  1204.7 70.9 reduce-scatter.11
  1284.3 34.0 all-gather.19
  1350.2 68.9 reduce-scatter.17
  1423.3 94.2 reduce-scatter.15
  1520.2 70.7 reduce-scatter.13
  1594.7 513.4 reduce-scatter.19
where the time goes:
time: 2200 us; the launch traced here: 2190 us
  waiting for transfers between devices  1590 us (72%)
  matrix products  218 us (10%)
  other arithmetic  212 us (10%)
  blocking collectives  128 us (6%)
  between operations  24.7 us (1%)
    all_gather x1, waiting for transfers between devices, local(): lax.all_gather(low_mlp, 'dp', axis=1, tiled=True)  606 us
    reduce_scatter x1, waiting for transfers between devices, local(): lax.psum_scatter(jnp.concatenate([grad_gate_up_w, grad_down[None]], 0).as...  470 us
    convert_element_type x3, other arithmetic, quantize(): ((sliced * spacing).astype(jnp.float32) * step_sizes).astype(jnp.bfloat16)  106 us
    unnamed x2, blocking collectives  88.2 us
    all_gather x1, waiting for transfers between devices, local(): lax.all_gather(low_qo, 'dp', axis=1, tiled=True)  71.8 us
    reduce_scatter x1, waiting for transfers between devices, local(): lax.psum_scatter(jnp.einsum('ktf,kdf->td', row_block, back_mlp[:2], prefe...  71 us
    reduce_scatter x1, waiting for transfers between devices, local(): lax.psum_scatter(contract_cols(row_block, full_mlp[2]), 'mp', scatter_dim...  70.9 us
    reduce_scatter x1, waiting for transfers between devices, local(): lax.psum_scatter(contract_cols(grad_query_lin, back_qo[0]) + contract_col...  70.1 us
  transfers between devices with their start and end apart: 14, of which 11 were waited for; matrix products, arithmetic and copies ran while one was open for 10% of the time, Pallas kernels for 0%

commit v1 on v0

--- a/solution.py
+++ b/solution.py
@@ -20,6 +20,27 @@
 WEIGHT_DECAY = 0.1
 ADAM_EPSILON = 1e-08
 CLIP_SCALE = 0.5
+
+
+def collect(x, axis, dim):
+    count, place, rows = (lax.axis_size(axis), lax.axis_index(axis), x.shape[dim])
+    right = [(i, (i + 1) % count) for i in range(count)]
+    downward = [(i, (i - 1) % count) for i in range(count)]
+    out = jnp.zeros((*x.shape[:dim], count * rows, *x.shape[dim + 1 :]), x.dtype)
+    out = lax.dynamic_update_slice_in_dim(out, x, place * rows, axis=dim)
+    from_left = from_right = x
+    half = count // 2
+    for step in range(1, half + 1):
+        from_left = lax.ppermute(from_left, axis, right)
+        out = lax.dynamic_update_slice_in_dim(
+            out, from_left, (place - step) % count * rows, axis=dim
+        )
+        if step < count - half:
+            from_right = lax.ppermute(from_right, axis, downward)
+            out = lax.dynamic_update_slice_in_dim(
+                out, from_right, (place + step) % count * rows, axis=dim
+            )
+    return out
 
 
 def quantize(master, fan_list, selector):
@@ -118,7 +139,7 @@
     low_kv = quantize(w_kv, (D, D), bit_sel[1])
     low_mlp = quantize(w_mlp, (D, D, FF), bit_sel[2])
     full_qo, full_kv, full_mlp = (
-        lax.all_gather(low_qo, "dp", axis=1, tiled=True),
+        collect(low_qo, "dp", 1),
         lax.all_gather(low_kv, "dp", axis=1, tiled=True),
         lax.all_gather(low_mlp, "dp", axis=1, tiled=True),
     )

time: 2200 us -> 2340 us (1.064)
  local copies, waits for them, and re-layouts: 20.8 us -> 106 us
  starting transfers between devices: 0.97 us -> 40.1 us
    dynamic_update_slice x0 -> x8, local copies, waits for them, and re-layouts: none -> 70.3 us  [the longest x4 35 us: collect(): lax.dynamic_update_slice_in_dim(out, from_left, (place - step) % count *...]
    ppermute x0 -> x7, waiting for transfers between devices: none -> 39.7 us  [the longest x4 39.7 us: collect(): from_left = lax.ppermute(from_left, axis, right)]
    ppermute x0 -> x7, starting transfers between devices: none -> 39.1 us  [the longest x3 29.3 us: collect(): from_right = lax.ppermute(from_right, axis, downward)]
  transfers between devices with their start and end apart: 14 -> 21, of which waited for: 11 -> 13; matrix products, arithmetic and copies ran while one was open for 10% -> 13% of each run, Pallas kernels for 0% -> 0%
where the time goes in v1:
time: 2340 us; the launch traced here: 2330 us
  waiting for transfers between devices  1610 us (69%)
  matrix products  217 us (9%)
  other arithmetic  210 us (9%)
  blocking collectives  128 us (5%)
  local copies, waits for them, and re-layouts  106 us (5%)
  starting transfers between devices  40.1 us (2%)
  between operations  24.9 us (1%)
    all_gather x1, waiting for transfers between devices, local(): lax.all_gather(low_mlp, 'dp', axis=1, tiled=True)  606 us
    reduce_scatter x1, waiting for transfers between devices, local(): lax.psum_scatter(jnp.concatenate([grad_gate_up_w, grad_down[None]], 0).as...  470 us
    convert_element_type x3, other arithmetic, quantize(): ((sliced * spacing).astype(jnp.float32) * step_sizes).astype(jnp.bfloat16)  106 us
    unnamed x2, blocking collectives  88.2 us
    all_gather x1, waiting for transfers between devices, local(): lax.all_gather(low_qo, 'dp', axis=1, tiled=True)  74.2 us
    reduce_scatter x1, waiting for transfers between devices, local(): lax.psum_scatter(contract_cols(row_block, full_mlp[2]), 'mp', scatter_dim...  70.8 us
    reduce_scatter x1, waiting for transfers between devices, local(): lax.psum_scatter(contract_cols(row_block, full_qo[1]), 'mp', scatter_dime...  70.6 us
    reduce_scatter x1, waiting for transfers between devices, local(): lax.psum_scatter(jnp.einsum('ktf,kdf->td', row_block, back_mlp[:2], prefe...  70.2 us
  transfers between devices with their start and end apart: 21, of which 13 were waited for; matrix products, arithmetic and copies ran while one was open for 13% of the time, Pallas kernels for 0%

profile of v1, /device:TPU:0, one launch (start us, length us, event | category | flops | bytes accessed | tf_op | source)
XLA Modules:
  0.0 2332.6 jit_solution(16436520585783709005)
XLA Ops:
  10.0 7.8 fusion.133
  18.9 43.8 %all-reduce.4 = f32[9216]{0:T(1024)S(1)} all-reduce(f32[9216]{0:T(1024)S(1)} %dynamic-update-slice), channel_id=1, replica_groups=mesh['dp'=8,'mp'=4] {'dp','mp'}, use_global_device_ids=true, to_apply=%add.4 | all-reduce | flops 9216 | bytes 73728
  67.9 13.7 fusion.105
  86.4 21.1 collective-permute-done
  107.5 2.6 collective-permute-start.2
  111.3 12.2 collective-permute-start.3
  123.5 10.1 collective-permute-done.2
  136.8 14.6 collective-permute-start.5
  151.4 8.4 collective-permute-done.4
  162.8 2.5 broadcast_in_dim.35
  165.3 7.9 dynamic_update_slice.24
  175.5 2.5 copy.80
  178.0 8.6 dynamic_update_slice.25
  188.8 9.1 dynamic_update_slice.26
  200.2 9.1 dynamic_update_slice.27
  211.5 9.1 dynamic_update_slice.28
  222.9 9.1 dynamic_update_slice.29
  234.2 9.1 dynamic_update_slice.30
  245.6 8.2 dynamic_update_slice.31
  253.8 3.2 slice.125
  257.0 4.1 fusion.113
  261.5 2.6 fusion.52
  264.3 3.4 fusion.115
  279.0 5.6 fusion.74
  284.7 70.6 %reduce-scatter.8.cloned.1.call-done = f32[224,2304]{1,0:T(8,128)} async-done(((f32[896,2304]{1,0:T(8,128)}), f32[224,2304]{1,0:T(8,128)}) %reduce-scatter.8.cloned.1.call-update) | async-done | bytes 2064400 | tf_op jit(solution)/shard_map/reduce_scatter | solution.py:192
  363.8 84.8 %fusion.33 = bf16[3,288,2304]{2,1,0:T(8,128)(2,1)} fusion(f32[3,288,2304]{2,1,0:T(8,128)} %param.27, f32[3]{0:T(128)S(1)} %copy-done.56, s32[]{:T(128)} %bitcast.23, s32[]{:T(128)S(6)} %sign.50, s32[]{:T(128)S(6)} %select_n.162, f32[3]{0:T(128)S(1)} %copy-done.57, s32[]{:T(128)S(6)} %neg.36, s32[]{:T(128)S(6)} %sub.146), kind=kLoop, calls=%fused_computation.52 | loop fusion | flops 39813120 | bytes 11943980 | tf_op jit(solution)/shard_map/convert_element_type | solution.py:55
  448.7 605.9 %all-gather.12.cloned.1.call-done = bf16[3,2304,2304]{2,1,0:T(8,128)(2,1)} async-done(((bf16[3,288,2304]{2,1,0:T(8,128)(2,1)}), bf16[3,2304,2304]{2,1,0:T(8,128)(2,1)}) %all-gather.12.cloned.1.call-update) | async-done | bytes 31850512 | tf_op jit(solution)/shard_map/all_gather | solution.py:144
  1054.5 28.8 %convolution_bitcast_fusion = f32[2,896,2304]{1,2,0:T(8,128)} fusion(bf16[3,2304,2304]{2,1,0:T(8,128)(2,1)} %all-gather.12.cloned.1.call-done, bf16[896,2304]{1,0:T(8,128)(2,1)} %all-gather.14.cloned.1.call-done), kind=kOutput, calls=%fused_computation.18 | convolution fusion | flops 19025362944 | bytes 52494336 | tf_op jit(solution)/shard_map/td,kdf->ktf/dot_general | solution.py:198
  1083.3 22.6 fusion.6
  1106.1 70.8 %reduce-scatter.10.cloned.1.call-done = f32[224,2304]{1,0:T(8,128)} async-done(((f32[896,2304]{1,0:T(8,128)}), f32[224,2304]{1,0:T(8,128)}) %reduce-scatter.10.cloned.1.call-update) | async-done | bytes 2064400 | tf_op jit(solution)/shard_map/reduce_scatter | solution.py:201
  1178.9 3.5 multiply_reduce_fusion
  1182.4 2.6 fusion.75
  1185.1 34.2 %all-gather.16.cloned.1.call-done = bf16[896,2304]{1,0:T(8,128)(2,1)} async-done(((bf16[224,2304]{1,0:T(8,128)(2,1)}), bf16[896,2304]{1,0:T(8,128)(2,1)}) %all-gather.16.cloned.1.call-update) | async-done | bytes 4128784 | tf_op jit(solution)/shard_map/all_gather | solution.py:211
  1219.3 26.8 %fusion.58 = (bf16[1,896,2304]{1,2,0:T(8,128)(2,1)}, bf16[1,896,2304]{1,2,0:T(8,128)(2,1)}) fusion(f32[2,896,2304]{1,2,0:T(8,128)} %convolution_bitcast_fusion, bf16[896,2304]{1,0:T(8,128)(2,1)} %all-gather.16.cloned.1.call-done, bf16[3,2304,2304]{2,1,0:T(8,128)(2,1)} %all-gather.12.cloned.1.call-done), kind=kOutput, calls=%fused_computation.87 | convolution fusion | flops 9562226688 | bytes 39518208 | tf_op jit(solution)/shard_map/dot_general | solution.py:217
  1246.1 27.1 %fusion.43 = f32[896,2304]{1,0:T(8,128)} fusion(bf16[3,2304,2304]{2,1,0:T(8,128)(2,1)} %all-gather.12.cloned.1.call-done, bf16[1,896,2304]{1,2,0:T(8,128)(2,1)} %get-tuple-element.39, bf16[1,896,2304]{1,2,0:T(8,128)(2,1)} %get-tuple-element.38), kind=kOutput, calls=%fused_computation.73 | convolution fusion | flops 19029491712 | bytes 37748736 | tf_op jit(solution)/shard_map/ktf,kdf->td/dot_general | solution.py:231
  1274.1 70.2 %reduce-scatter.12.cloned.1.call-done = f32[224,2304]{1,0:T(8,128)} async-done(((f32[896,2304]{1,0:T(8,128)}), f32[224,2304]{1,0:T(8,128)}) %reduce-scatter.12.cloned.1.call-update) | async-done | bytes 2064400 | tf_op jit(solution)/shard_map/reduce_scatter | solution.py:230
  1347.1 2.9 multiply_reduce_fusion.2
  1352.8 74.2 %all-gather.20.cloned.1.call-done = bf16[2,2304,512]{2,1,0:T(8,128)(2,1)} async-done(((bf16[2,288,512]{2,1,0:T(8,128)(2,1)}), bf16[2,2304,512]{2,1,0:T(8,128)(2,1)}) %all-gather.20.cloned.1.call-update) | async-done | bytes 4718608 | tf_op jit(solution)/shard_map/all_gather | solution.py:213
  1427.0 34.3 %all-gather.18.cloned.1.call-done = bf16[896,2304]{1,0:T(8,128)(2,1)} async-done(((bf16[224,2304]{1,0:T(8,128)(2,1)}), bf16[896,2304]{1,0:T(8,128)(2,1)}) %all-gather.18.cloned.1.call-update) | async-done | bytes 4128784 | tf_op jit(solution)/shard_map/all_gather | solution.py:241
  1461.3 5.6 fusion.84
  1466.9 5.5 fusion.41
  1472.4 5.4 fusion.97
  1477.8 2.9 fusion.40
  1480.8 3.8 fusion.124
  1484.7 3.6 fusion.123
  1493.0 3.0 bitcast_multiply_fusion.7
  1498.7 2.9 fusion.60
  1501.6 3.0 fusion.59
  1504.6 2.6 pad_maximum_fusion.4
  1507.5 2.6 fusion.112
  1510.1 4.2 fusion.72
  1514.3 4.5 add_add_fusion
  1518.9 20.8 fusion.3
  1539.7 29.3 %fusion.2 = bf16[2,2304,2304]{2,1,0:T(8,128)(2,1)} fusion(bf16[1,896,2304]{1,2,0:T(8,128)(2,1)} %get-tuple-element.39, bf16[1,896,2304]{1,2,0:T(8,128)(2,1)} %get-tuple-element.38, bf16[896,2304]{1,0:T(8,128)(2,1)S(1)} %copy-done.63), kind=kOutput, calls=%fused_computation.4 | convolution fusion | flops 19052494848 | bytes 33619968 | tf_op jit(solution)/shard_map/ktf,td->kdf/dot_general | solution.py:226
  1569.1 22.1 pad_maximum_fusion
  1593.6 66.7 %reduce-scatter.16.cloned.1.call-done = bf16[2,288,512]{2,1,0:T(8,128)(2,1)} async-done(((bf16[2,2304,512]{2,1,0:T(8,128)(2,1)}), bf16[2,288,512]{2,1,0:T(8,128)(2,1)}) %reduce-scatter.16.cloned.1.call-update) | async-done | bytes 589840 | tf_op jit(solution)/shard_map/reduce_scatter | solution.py:285
  1663.7 70.1 %reduce-scatter.14.cloned.1.call-done = f32[224,2304]{1,0:T(8,128)} async-done(((f32[896,2304]{1,0:T(8,128)}), f32[224,2304]{1,0:T(8,128)}) %reduce-scatter.14.cloned.1.call-update) | async-done | bytes 2064400 | tf_op jit(solution)/shard_map/reduce_scatter | solution.py:273
  1735.9 44.4 %all-reduce.5 = f32[9216]{0:T(1024)S(1)} all-reduce(f32[9216]{0:T(1024)S(1)} %reshape.540), channel_id=9, replica_groups=mesh['dp'=8,'mp'=4] {'dp','mp'}, use_global_device_ids=true, to_apply=%region_27.28.clone | all-reduce | flops 9216 | bytes 73728
  1781.0 470.1 %reduce-scatter.20.cloned.1.call-done = bf16[3,288,2304]{2,1,0:T(8,128)(2,1)} async-done(((bf16[3,2304,2304]{2,1,0:T(8,128)(2,1)}), bf16[3,288,2304]{2,1,0:T(8,128)(2,1)}) %reduce-scatter.20.cloned.1.call-update) | async-done | bytes 3981328 | tf_op jit(solution)/shard_map/reduce_scatter | solution.py:297
  2251.1 4.8 fusion.27
  2257.3 4.1 fusion.78
  2261.4 39.7 %psum.7 = f32[]{:T(128)} all-reduce(f32[]{:T(128)S(6)} %add.378), channel_id=1, replica_groups=mesh['dp'=8,'mp'=4] {'dp','mp'}, use_global_device_ids=true, to_apply=%region_29.30 | all-reduce | flops 1 | bytes 8 | tf_op jit(solution)/shard_map/psum | solution.py:314
  2302.5 4.1 multiply_subtract_fusion.1
  2308.1 16.3 multiply_subtract_fusion
  (255 shorter events, 77.8 us)
Async XLA Ops:
  7.2 60.7 %copy-start.58 = (f32[2]{0:T(128)S(1)}, f32[2]{0:T(128)}, u32[]{:S(2)}) copy-start(f32[2]{0:T(128)} %constant.277) | copy-start | bytes 28
  7.2 60.7 %copy-start.59 = (f32[2]{0:T(128)S(1)}, f32[2]{0:T(128)}, u32[]{:S(2)}) copy-start(f32[2]{0:T(128)} %constant.263.clone) | copy-start | bytes 28
  7.2 57.9 %copy-start = (f32[224,2304]{1,0:T(8,128)S(1)}, f32[224,2304]{1,0:T(8,128)}, u32[]{:S(2)}) copy-start(f32[224,2304]{1,0:T(8,128)} %param.20) | copy-start | bytes 6193156
  7.2 249.8 %all-gather.10.cloned.1.call-start = ((), (), s32[]{:S(2)}) async-start(), calls=%async_computation.8 | async-start | bytes 2654208 | tf_op jit(solution)/shard_map/all_gather | solution.py:143
  17.9 239.1 %all-gather.8.cloned.1.call-start = ((), (), s32[]{:S(2)}) async-start(), calls=%async_computation.7 | async-start | bytes 5160960 | tf_op jit(solution)/shard_map/all_gather | solution.py:156
  17.9 92.1 %copy-start.45 = (s32[1,896]{1,0:T(1,128)S(1)}, s32[1,896]{1,0:T(1,128)}, u32[]{:S(2)}) copy-start(s32[1,896]{1,0:T(1,128)} %param.22) | copy-start | bytes 10756
  18.9 117.9 %copy-start.53 = (s32[1,896]{1,0:T(1,128)S(1)}, s32[1,896]{1,0:T(1,128)}, u32[]{:S(2)}) copy-start(s32[1,896]{1,0:T(1,128)} %param.23) | copy-start | bytes 10756
  64.5 293.2 %copy-start.36 = (f32[2304]{0:T(1024)}, f32[2304]{0:T(1024)S(1)}, u32[]{:S(2)}) copy-start(f32[2304]{0:T(1024)S(1)} %get-tuple-element.55) | copy-start | bytes 27652
  66.3 289.0 %reduce-scatter.8.cloned.1.call-start = ((), (), s32[]{:S(2)}) async-start(), calls=%async_computation.9 | async-start | bytes 10321920 | tf_op jit(solution)/shard_map/reduce_scatter | solution.py:192
  81.6 91.6 %copy-start.17 = (bf16[2,288,512]{2,1,0:T(8,128)(2,1)}, bf16[2,288,512]{2,1,0:T(8,128)(2,1)S(1)}, u32[]{:S(2)}) copy-start(bf16[2,288,512]{2,1,0:T(8,128)(2,1)S(1)} %fusion.105) | copy-start | bytes 1769476
  81.6 25.9 %collective-permute-start = (bf16[2,288,512]{2,1,0:T(8,128)(2,1)S(1)}, bf16[2,288,512]{2,1,0:T(8,128)(2,1)}, u32[]{:S(2)}, u32[]{:S(2)}) collective-permute-start(bf16[2,288,512]{2,1,0:T(8,128)(2,1)S(1)} %fusion.105), channel_id=1, source_target_pairs={{0,4},{4,8},{8,12},{12,16},{16,20},{20,24},{24,28},{28,0},{1,5},{5... | collective-permute-start | bytes 1769480 | tf_op jit(solution)/shard_map/ppermute | solution.py:34
  83.9 27.3 %collective-permute-start.1 = (bf16[2,288,512]{2,1,0:T(8,128)(2,1)S(1)}, bf16[2,288,512]{2,1,0:T(8,128)(2,1)S(1)}, u32[]{:S(2)}, u32[]{:S(2)}) collective-permute-start(bf16[2,288,512]{2,1,0:T(8,128)(2,1)S(1)} %fusion.105), channel_id=1, source_target_pairs={{0,28},{4,0},{8,4},{12,8},{16,12},{20,16},{24,20},{28,24},{1,29},{... | collective-permute-start | bytes 1769480 | tf_op jit(solution)/shard_map/ppermute | solution.py:39
  107.5 26.2 %collective-permute-start.2 = (bf16[2,288,512]{2,1,0:T(8,128)(2,1)}, bf16[2,288,512]{2,1,0:T(8,128)(2,1)}, u32[]{:S(2)}, u32[]{:S(2)}) collective-permute-start(bf16[2,288,512]{2,1,0:T(8,128)(2,1)} %collective-permute-done), channel_id=1, source_target_pairs={{0,4},{4,8},{8,12},{12,16},{16,20},{20,24},{24,28},{28,0},{1,5},{5... | collective-permute-start | bytes 1769480 | tf_op jit(solution)/shard_map/ppermute | solution.py:34
  111.3 51.0 %copy-start.31 = (bf16[2,288,512]{2,1,0:T(8,128)(2,1)}, bf16[2,288,512]{2,1,0:T(8,128)(2,1)S(1)}, u32[]{:S(2)}) copy-start(bf16[2,288,512]{2,1,0:T(8,128)(2,1)S(1)} %collective-permute-done.1) | copy-start | bytes 1769476
  111.3 25.5 %collective-permute-start.3 = (bf16[2,288,512]{2,1,0:T(8,128)(2,1)S(1)}, bf16[2,288,512]{2,1,0:T(8,128)(2,1)}, u32[]{:S(2)}, u32[]{:S(2)}) collective-permute-start(bf16[2,288,512]{2,1,0:T(8,128)(2,1)S(1)} %collective-permute-done.1), channel_id=1, source_target_pairs={{0,28},{4,0},{8,4},{12,8},{16,12},{20,16},{24,20},{28,24},{1,29},{... | collective-permute-start | bytes 1769480 | tf_op jit(solution)/shard_map/ppermute | solution.py:39
  133.7 26.2 %collective-permute-start.4 = (bf16[2,288,512]{2,1,0:T(8,128)(2,1)}, bf16[2,288,512]{2,1,0:T(8,128)(2,1)}, u32[]{:S(2)}, u32[]{:S(2)}) collective-permute-start(bf16[2,288,512]{2,1,0:T(8,128)(2,1)} %collective-permute-done.2), channel_id=1, source_target_pairs={{0,4},{4,8},{8,12},{12,16},{16,20},{20,24},{24,28},{28,0},{1,5},{5... | collective-permute-start | bytes 1769480 | tf_op jit(solution)/shard_map/ppermute | solution.py:34
  136.8 95.2 %collective-permute-start.5 = (bf16[2,288,512]{2,1,0:T(8,128)(2,1)}, bf16[2,288,512]{2,1,0:T(8,128)(2,1)}, u32[]{:S(2)}, u32[]{:S(2)}) collective-permute-start(bf16[2,288,512]{2,1,0:T(8,128)(2,1)} %collective-permute-done.3), channel_id=1, source_target_pairs={{0,28},{4,0},{8,4},{12,8},{16,12},{20,16},{24,20},{28,24},{1,29},{... | collective-permute-start | bytes 1769480 | tf_op jit(solution)/shard_map/ppermute | solution.py:39
  159.8 83.6 %collective-permute-start.6 = (bf16[2,288,512]{2,1,0:T(8,128)(2,1)}, bf16[2,288,512]{2,1,0:T(8,128)(2,1)}, u32[]{:S(2)}, u32[]{:S(2)}) collective-permute-start(bf16[2,288,512]{2,1,0:T(8,128)(2,1)} %collective-permute-done.4), channel_id=1, source_target_pairs={{0,4},{4,8},{8,12},{12,16},{16,20},{20,24},{24,28},{28,0},{1,5},{5... | collective-permute-start | bytes 1769480 | tf_op jit(solution)/shard_map/ppermute | solution.py:34
  175.5 100.1 %copy-start.15 = (pred[896,896]{0,1:T(8,128)(4,1)}, pred[896,896]{0,1:T(8,128)(4,1)S(1)}, u32[]{:S(2)}) copy-start(pred[896,896]{0,1:T(8,128)(4,1)S(1)} %fusion.70) | copy-start | bytes 2408452
  257.0 4.5 copy-start.60
  270.9 4.7 copy-start.6
  274.4 4.7 slice-start.2
  284.6 164.0 %all-gather.14.cloned.1.call-start = ((), (), s32[]{:S(2)}) async-start(), calls=%async_computation.11 | async-start | bytes 5160960 | tf_op jit(solution)/shard_map/all_gather | solution.py:197
  357.7 6.1 copy-start.56
  357.7 6.1 copy-start.57
  359.8 88.7 %copy-start.50 = (f32[224]{0:T(256)}, f32[224]{0:T(256)S(1)}, u32[]{:S(2)}) copy-start(f32[224]{0:T(256)S(1)} %get-tuple-element.36) | copy-start | bytes 2692
  362.4 692.2 %all-gather.12.cloned.1.call-start = ((), (), s32[]{:S(2)}) async-start(), calls=%async_computation.10 | async-start | bytes 35831808 | tf_op jit(solution)/shard_map/all_gather | solution.py:144
  448.6 728.4 %reduce-scatter.10.cloned.1.call-start = ((), (), s32[]{:S(2)}) async-start(), calls=%async_computation.12 | async-start | bytes 10321920 | tf_op jit(solution)/shard_map/reduce_scatter | solution.py:201
  1106.0 76.5 %copy-start.3 = (f32[224,2304]{1,0:T(8,128)S(1)}, f32[224,2304]{1,0:T(8,128)}, u32[]{:S(2)}) copy-start(f32[224,2304]{1,0:T(8,128)} %copy-done.2) | copy-start | bytes 6193156
  1106.0 113.4 %all-gather.16.cloned.1.call-start = ((), (), s32[]{:S(2)}) async-start(), calls=%async_computation.13 | async-start | bytes 5160960 | tf_op jit(solution)/shard_map/all_gather | solution.py:211
  1176.9 5.5 copy-start.8
  1176.9 5.5 copy-start.9
  1185.1 159.2 %reduce-scatter.12.cloned.1.call-start = ((), (), s32[]{:S(2)}) async-start(), calls=%async_computation.14 | async-start | bytes 10321920 | tf_op jit(solution)/shard_map/reduce_scatter | solution.py:230
  1273.3 73.3 %copy-start.51 = (f32[224]{0:T(256)S(1)}, f32[224]{0:T(256)}, u32[]{:S(2)}) copy-start(f32[224]{0:T(256)} %copy-done.50) | copy-start | bytes 2692
  1273.3 73.3 %copy-start.37 = (f32[2304]{0:T(1024)S(1)}, f32[2304]{0:T(1024)}, u32[]{:S(2)}) copy-start(f32[2304]{0:T(1024)} %copy-done.36) | copy-start | bytes 27652
  1273.3 73.3 %copy-start.44 = (f32[224]{0:T(256)S(1)}, f32[224]{0:T(256)}, u32[]{:S(2)}) copy-start(f32[224]{0:T(256)} %copy-done.43) | copy-start | bytes 2692
  1273.3 153.7 %all-gather.20.cloned.1.call-start = ((), (), s32[]{:S(2)}) async-start(), calls=%async_computation.16 | async-start | bytes 5308416 | tf_op jit(solution)/shard_map/all_gather | solution.py:213
  1274.0 187.2 %all-gather.18.cloned.1.call-start = ((), (), s32[]{:S(2)}) async-start(), calls=%async_computation.15 | async-start | bytes 5160960 | tf_op jit(solution)/shard_map/all_gather | solution.py:241
  1352.8 114.1 %copy-start.16 = (pred[896,896]{0,1:T(8,128)(4,1)S(1)}, pred[896,896]{0,1:T(8,128)(4,1)}, u32[]{:S(2)}) copy-start(pred[896,896]{0,1:T(8,128)(4,1)} %copy-done.15) | copy-start | bytes 2408452
  1352.8 114.1 %copy-start.40 = (f32[2,896]{1,0:T(2,128)S(1)}, f32[2,896]{1,0:T(2,128)}, u32[]{:S(2)}) copy-start(f32[2,896]{1,0:T(2,128)} %copy-done.39) | copy-start | bytes 21508
  1352.8 114.1 %copy-start.68 = (bf16[896,256,1]{1,0,2:T(8,128)(2,1)S(1)}, bf16[896,256,1]{1,0,2:T(8,128)(2,1)}, u32[]{:S(2)}) copy-start(bf16[896,256,1]{1,0,2:T(8,128)(2,1)} %copy-done.67) | copy-start | bytes 1376260
  1352.8 239.1 %reduce-scatter.18.cloned.1.call-start = ((), (), s32[]{:S(2)}) async-start(), calls=%async_computation.19 | async-start | bytes 2654208 | tf_op jit(solution)/shard_map/reduce_scatter | solution.py:291
  1466.8 10.9 slice-start
  1466.9 10.9 slice-start.1
  1477.8 10.5 copy-start.32
  1480.8 7.5 copy-start.61
  1492.9 167.5 %reduce-scatter.16.cloned.1.call-start = ((), (), s32[]{:S(2)}) async-start(), calls=%async_computation.18 | async-start | bytes 5308416 | tf_op jit(solution)/shard_map/reduce_scatter | solution.py:285
  1507.2 226.5 %reduce-scatter.14.cloned.1.call-start = ((), (), s32[]{:S(2)}) async-start(), calls=%async_computation.17 | async-start | bytes 10321920 | tf_op jit(solution)/shard_map/reduce_scatter | solution.py:273
  1510.0 4.2 copy-start.23
  1510.1 4.2 copy-start.33
  1518.9 732.3 %reduce-scatter.20.cloned.1.call-start = ((), (), s32[]{:S(2)}) async-start(), calls=%async_computation.20 | async-start | bytes 35831808 | tf_op jit(solution)/shard_map/reduce_scatter | solution.py:297
  1518.9 20.8 copy-start.63
  1591.1 142.6 %copy-start.1 = (f32[224,2304]{1,0:T(8,128)S(1)}, f32[224,2304]{1,0:T(8,128)}, u32[]{:S(2)}) copy-start(f32[224,2304]{1,0:T(8,128)} %param.20) | copy-start | bytes 6193156
  1591.1 142.6 %copy-start.35 = (f32[2304]{0:T(1024)S(1)}, f32[2304]{0:T(1024)}, u32[]{:S(2)}) copy-start(f32[2304]{0:T(1024)} %copy-done.34) | copy-start | bytes 27652
  1591.2 142.6 %copy-start.42 = (f32[224]{0:T(256)S(1)}, f32[224]{0:T(256)}, u32[]{:S(2)}) copy-start(f32[224]{0:T(256)} %copy-done.41) | copy-start | bytes 2692
  1591.2 189.8 %copy-start.47 = (f32[224]{0:T(256)S(1)}, f32[224]{0:T(256)}, u32[]{:S(2)}) copy-start(f32[224]{0:T(256)} %copy-done.46) | copy-start | bytes 2692
  2257.2 44.6 %copy-start.52 = (f32[288]{0:T(512)S(1)}, f32[288]{0:T(512)}, u32[]{:S(2)}) copy-start(f32[288]{0:T(512)} %param.28) | copy-start | bytes 3460
  2257.2 44.6 %copy-start.54 = (f32[288]{0:T(512)S(1)}, f32[288]{0:T(512)}, u32[]{:S(2)}) copy-start(f32[288]{0:T(512)} %param.36) | copy-start | bytes 3460
  2257.2 44.6 %copy-start.55 = (f32[288]{0:T(512)S(1)}, f32[288]{0:T(512)}, u32[]{:S(2)}) copy-start(f32[288]{0:T(512)} %param.32) | copy-start | bytes 3460
  2257.2 45.3 %copy-start.18 = (f32[2,288,512]{2,1,0:T(8,128)S(1)}, f32[2,288,512]{2,1,0:T(8,128)}, u32[]{:S(2)}) copy-start(f32[2,288,512]{2,1,0:T(8,128)} %param.25) | copy-start | bytes 3538948
  2261.4 45.3 %copy-start.25 = (f32[2,288,256]{2,1,0:T(8,128)S(1)}, f32[2,288,256]{2,1,0:T(8,128)}, u32[]{:S(2)}) copy-start(f32[2,288,256]{2,1,0:T(8,128)} %param.26) | copy-start | bytes 1769476
  2261.4 45.3 %copy-start.28 = (bf16[2,288,256]{2,1,0:T(8,128)(2,1)S(1)}, bf16[2,288,256]{2,1,0:T(8,128)(2,1)}, u32[]{:S(2)}) copy-start(bf16[2,288,256]{2,1,0:T(8,128)(2,1)} %reduce-scatter.18.cloned.1.call-done) | copy-start | bytes 884740
  2261.4 45.3 %copy-start.29 = (f32[2,288,256]{2,1,0:T(8,128)S(1)}, f32[2,288,256]{2,1,0:T(8,128)}, u32[]{:S(2)}) copy-start(f32[2,288,256]{2,1,0:T(8,128)} %param.34) | copy-start | bytes 1769476
  2261.4 45.3 %copy-start.30 = (f32[2,288,256]{2,1,0:T(8,128)S(1)}, f32[2,288,256]{2,1,0:T(8,128)}, u32[]{:S(2)}) copy-start(f32[2,288,256]{2,1,0:T(8,128)} %param.30) | copy-start | bytes 1769476
  (30 other events, 66.9 us)
Sparse Core Ops, SparseCore 0:
  18.0 55.5 all-gather.9
  75.8 32.6 all-gather.7
  284.8 70.5 reduce-scatter.7
  362.5 34.2 all-gather.13
  448.7 605.7 all-gather.11
  1106.1 70.8 reduce-scatter.9
  1185.2 34.1 all-gather.15
  1273.4 70.8 reduce-scatter.11
  1347.1 79.8 all-gather.19
  1429.0 32.2 all-gather.17
  1493.0 68.9 reduce-scatter.17
  1566.1 94.2 reduce-scatter.15
  1663.0 70.6 reduce-scatter.13
  1737.5 513.5 reduce-scatter.19
